TPU v7x, 512 devices: a whole 4x4x16 slice. The times are simulated.
512 devices in a mesh: kgrp: 16 (over y_hi, x, core), band: 32 (over z, y_lo).
Axes of the slice: x: 4, y: 4 (y_hi: 2, y_lo: 2; y = y_hi * 2 + y_lo), z: 16, core: 2. Of those that a mesh axis runs over, the one named last changes fastest.
Arguments:
- orbitals: bfloat16 [16, 128, 2, 32768], P('kgrp', 'band'), may hold values from -6 to 6
- points: int32 [512], replicated, may hold values from 0 to 32767, as said below
- partner: int32 [16], replicated, may hold values from 0 to 15, each once
- coulomb: bfloat16 [512, 32768], P(None, 'band'), may hold values from -0.01171875 to 0.01171875
Outputs:
- exchange_term: bfloat16 [16, 128, 2, 32768], P('kgrp', 'band')
Inputs may be any that keep to these rules, and one draw needn't show every extreme that they name: `points`: 512 distinct grid cells; cells 0 and 32767 are always among them.
All inputs are finite; a program needn't handle non-finite values.
Results may differ from a plain program's by a relative error of at most 0.0057.
Values may be sent and summed in bfloat16 or wider, within the bound.
A program may use at most 64 MiB of HBM per device.

v0:
```python
import math

import jax
import jax.numpy as jnp
from jax import lax
from jax.sharding import PartitionSpec as P

GX = 32
GY = 32
GZ = 32


def matched_values(own_block, partner):
    my_group = lax.axis_index("kgrp")
    shard_rows = lax.all_gather(own_block[None], "kgrp", axis=0, tiled=True)
    chosen = partner == my_group
    kept = jnp.where(chosen[:, None, None, None], shard_rows, jnp.zeros_like(shard_rows))
    return jnp.sum(kept, axis=0)


def axis_table(length):
    index = jnp.arange(length, dtype=jnp.int32)
    phase = 2.0 * math.pi / length * (index[:, None] * index[None, :] % length).astype(jnp.float32)
    cos_t = jnp.cos(phase) / math.sqrt(length)
    sin_t = jnp.sin(phase) / math.sqrt(length)
    from_real = jnp.stack([cos_t, -sin_t], axis=1)
    from_imag = jnp.stack([sin_t, cos_t], axis=1)
    return jnp.stack([from_real, from_imag], axis=0)


def axis_pass(field, length, form):
    return jnp.einsum(form, field, axis_table(length), precision=lax.Precision.HIGHEST)


def body(orbitals, points, partner, coulomb):
    resident = orbitals[0]
    band_rows = resident.shape[0]
    slices = lax.all_to_all(resident, "band", split_axis=2, concat_axis=0, tiled=True)
    band_index = lax.axis_index("band")
    cells = slices.shape[2]
    positions = band_index * cells + jnp.arange(cells, dtype=jnp.int32)
    selector = (positions[:, None] == points[None, :]).astype(jnp.bfloat16)
    picked_part = jnp.einsum("icr,rm->icm", slices, selector, preferred_element_type=jnp.float32)
    own_vals = lax.psum(picked_part.astype(jnp.bfloat16), "band")
    own_block = lax.dynamic_slice_in_dim(own_vals, band_index * band_rows, band_rows, 0)
    src_block = matched_values(own_block, partner)
    src_vals = lax.all_gather(src_block, "band", axis=0, tiled=True)
    turned = jnp.stack([-own_vals[:, 1], own_vals[:, 0]], axis=1)
    own_coef = jnp.stack([own_vals, turned], axis=2)
    density = jnp.einsum("icqm,icr->qmr", own_coef, slices, preferred_element_type=jnp.float32)
    weighted = (coulomb.astype(jnp.float32)[None] * density).astype(jnp.bfloat16)
    src_re = src_vals[:, 0]
    src_im = src_vals[:, 1]
    src_coef = -jnp.stack(
        [jnp.stack([src_re, -src_im], axis=1), jnp.stack([src_im, src_re], axis=1)], axis=1
    )
    on_grid = jnp.einsum(
        "ipqm,qmr->ipr", src_coef, weighted, preferred_element_type=jnp.float32
    ).astype(jnp.bfloat16)
    band_count = lax.axis_size("band")
    sendgrid = on_grid.reshape(band_count, band_rows, 2, cells)
    shards = lax.all_to_all(sendgrid, "band", split_axis=0, concat_axis=3, tiled=True)
    inner_rows = shards.shape[1]
    field = shards.astype(jnp.float32).reshape(inner_rows, 2, GX, GY, GZ)
    field = axis_pass(field, GX, "bcxyz,cxdk->bdkyz")
    field = axis_pass(field, GY, "bcxyz,cydk->bdxkz")
    field = axis_pass(field, GZ, "bcxyz,czdk->bdxyk")
    return field.reshape(1, inner_rows, 2, GX * GY * GZ).astype(jnp.bfloat16)


def solution(mesh):
    return jax.shard_map(
        body,
        mesh=mesh,
        in_specs=(P("kgrp", "band", None, None), P(), P(), P(None, "band")),
        out_specs=P("kgrp", "band", None, None),
        check_vma=False,
    )
```

profile of v0, /device:TPU:8, one launch (start us, length us, event | category | flops | bytes accessed | tf_op | source)
XLA Modules:
  0.0 625.4 jit_solution(913066813591795610)
XLA Ops:
  6.5 30.2 %copy.32 = bf16[1,4,2,32768]{1,2,3,0:T(2,128)(2,1)} copy(bf16[1,4,2,32768]{3,2,1,0:T(2,128)(2,1)} %param.4) | data formatting | bytes 1048576 | tf_op args[0]
  36.8 14.1 %bitcast_bitcast_fusion = bf16[32768,2,4]{2,1,0:T(2,128)(2,1)} fusion(bf16[1,4,2,32768]{1,2,3,0:T(2,128)(2,1)} %copy.32), kind=kLoop, calls=%fused_computation.61 | loop fusion | bytes 1048576
  50.9 31.8 %reshape.126 = bf16[32,2,4096]{2,1,0:T(2,128)(2,1)} reshape(bf16[32768,2,4]{2,1,0:T(2,128)(2,1)} %bitcast_bitcast_fusion) | data formatting | bytes 1048576
  82.7 16.7 %all-to-all-start = ((bf16[32,2,4096]{2,1,0:T(2,128)(2,1)}), bf16[32,2,4096]{2,1,0:T(2,128)(2,1)S(1)}, u32[]{:S(2)}, u32[]{:S(2)}) async-start(bf16[32,2,4096]{2,1,0:T(2,128)(2,1)} %reshape.126), calls=%async_computation | async-start | bytes 1048576 | tf_op jit(solution)/shard_map/all_to_all | solution.py:38
  99.5 32.6 %all-to-all-done = bf16[32,2,4096]{2,1,0:T(2,128)(2,1)S(1)} async-done(((bf16[32,2,4096]{2,1,0:T(2,128)(2,1)}), bf16[32,2,4096]{2,1,0:T(2,128)(2,1)S(1)}, u32[]{:S(2)}, u32[]{:S(2)}) %all-to-all-start) | async-done | bytes 524320 | tf_op jit(solution)/shard_map/all_to_all | solution.py:38
  132.2 37.1 %reshape.127 = bf16[32768,2,4]{2,1,0:T(2,128)(2,1)} reshape(bf16[32,2,4096]{2,1,0:T(2,128)(2,1)S(1)} %all-to-all-done) | data formatting | bytes 1048576
  169.3 35.0 %copy.33 = bf16[4,2,32,1024]{3,0,2,1:T(4,128)(2,1)S(1)} copy(bf16[4,2,32,1024]{0,1,3,2:T(2,128)(2,1)} %bitcast.110) | data formatting | bytes 1048576 | tf_op jit(solution)/shard_map/all_to_all | solution.py:38
  204.3 0.1 all_to_all.27
  204.5 1.2 fusion.26
  205.7 1.5 convert_element_type.65
  207.2 0.1 reshape.113
  207.3 254.8 %all-reduce.2.cloned.1.call-done = bf16[128,2,512]{0,2,1:T(8,128)(2,1)} async-done(((bf16[128,2,512]{0,2,1:T(8,128)(2,1)}), bf16[128,2,512]{0,2,1:T(8,128)(2,1)}) %all-reduce.2.cloned.1.call-update) | async-done | bytes 262160 | tf_op jit(solution)/shard_map/psum | solution.py:44
  462.1 1.2 constant_dynamic-slice_fusion
  463.2 0.1 copy.34
  463.4 23.5 %all-gather = bf16[64,2,512]{2,1,0:T(2,128)(2,1)S(1)} all-gather(bf16[4,2,512]{2,1,0:T(2,128)(2,1)S(1)} %copy.34), channel_id=2, replica_groups=mesh['kgrp'=16,'band'=32] {'kgrp'}, dimensions={0}, use_global_device_ids=true | all-gather | bytes 139264 | tf_op jit(solution)/shard_map/all_gather | solution.py:15
  486.9 0.1 fusion.39
  487.0 61.5 %all_gather.7 = bf16[128,2,512]{2,1,0:T(2,128)(2,1)S(1)} all-gather(bf16[4,2,512]{2,1,0:T(2,128)(2,1)S(1)} %fusion.39), channel_id=1, replica_groups=mesh['kgrp'=16,'band'=32] {'band'}, dimensions={0}, use_global_device_ids=true | all-gather | bytes 270336 | tf_op jit(solution)/shard_map/all_gather | solution.py:47
  548.6 0.4 fusion.56
  549.0 1.0 slice_negate_fusion
  550.0 0.7 maximum_bitcast_fusion.2
  550.8 3.0 fusion.20
  553.8 1.2 reshape.109
  555.0 1.1 copy.37
  556.1 11.5 %all-to-all-start.1 = ((bf16[32,4,2,1024]{3,1,2,0:T(4,128)(2,1)}), bf16[32,4,2,1024]{3,1,2,0:T(4,128)(2,1)S(1)}, u32[]{:S(2)}, u32[]{:S(2)}) async-start(bf16[32,4,2,1024]{3,1,2,0:T(4,128)(2,1)} %copy.37), calls=%async_computation.1 | async-start | bytes 1048576 | tf_op jit(solution)/shard_map/all_to_all | solution.py:62
  567.7 0.1 sine_multiply_fusion
  567.8 22.7 %all-to-all-done.1 = bf16[32,4,2,1024]{3,1,2,0:T(4,128)(2,1)S(1)} async-done(((bf16[32,4,2,1024]{3,1,2,0:T(4,128)(2,1)}), bf16[32,4,2,1024]{3,1,2,0:T(4,128)(2,1)S(1)}, u32[]{:S(2)}, u32[]{:S(2)}) %all-to-all-start.1) | async-done | bytes 524320 | tf_op jit(solution)/shard_map/all_to_all | solution.py:62
  590.5 1.2 reshape.125
  591.6 2.7 convolution_bitcast_fusion
  594.4 6.2 fusion.2
  600.6 10.7 %fusion.14 = bf16[4,2,32,32,32]{3,4,2,0,1:T(8,128)(2,1)S(1)} fusion(f32[2,32,4,32,32,1]{4,1,5,0,3,2:T(8,128)S(1)} %fusion.2, f32[1,32,2,32]{1,3,0,2:T(8,128)S(1)} %get-tuple-element.14, f32[1,32,2,32]{1,3,0,2:T(8,128)S(1)} %get-tuple-element.13), kind=kOutput, calls=%fused_computation.15 | convolution fusion | flops 201592832 | bytes 1589248 | tf_op jit(solution)/shard_map/bcxyz,czdk->bdxyk/dot_general | solution.py:32
  611.4 2.6 copy.41
  614.0 4.5 convert_element_type.70
  (15 shorter events, 0.3 us)
Async XLA Ops:
  82.7 49.4 %all-to-all-start = ((bf16[32,2,4096]{2,1,0:T(2,128)(2,1)}), bf16[32,2,4096]{2,1,0:T(2,128)(2,1)S(1)}, u32[]{:S(2)}, u32[]{:S(2)}) async-start(bf16[32,2,4096]{2,1,0:T(2,128)(2,1)} %reshape.126), calls=%async_computation | async-start | bytes 1048576 | tf_op jit(solution)/shard_map/all_to_all | solution.py:38
  99.5 362.6 %all-reduce.2.cloned.1.call-start = ((), (), s32[]{:S(2)}) async-start(), calls=%async_computation.2 | async-start | bytes 524288 | tf_op jit(solution)/shard_map/psum | solution.py:44
  169.3 35.2 %copy-start.1 = (s32[512]{0:T(512)S(1)}, s32[512]{0:T(512)}, u32[]{:S(2)}) copy-start(s32[512]{0:T(512)} %param.5) | copy-start | bytes 6148
  204.3 2.9 copy-start.2
  462.1 88.7 %copy-start = (bf16[128,2,512]{0,2,1:T(8,128)(2,1)S(1)}, bf16[128,2,512]{0,2,1:T(8,128)(2,1)}, u32[]{:S(2)}) copy-start(bf16[128,2,512]{0,2,1:T(8,128)(2,1)} %all-reduce.2.cloned.1.call-done) | copy-start | bytes 786436
  556.1 34.4 %all-to-all-start.1 = ((bf16[32,4,2,1024]{3,1,2,0:T(4,128)(2,1)}), bf16[32,4,2,1024]{3,1,2,0:T(4,128)(2,1)S(1)}, u32[]{:S(2)}, u32[]{:S(2)}) async-start(bf16[32,4,2,1024]{3,1,2,0:T(4,128)(2,1)} %copy.37), calls=%async_computation.1 | async-start | bytes 1048576 | tf_op jit(solution)/shard_map/all_to_all | solution.py:62
Sparse Core Ops, SparseCore 0:
  205.8 256.2 all-reduce.1
where the time goes:
time: 629 us; the launch traced here: 625 us
  waiting for transfers between devices  310 us (49%)
  local copies, waits for them, and re-layouts  161 us (26%)
  blocking collectives  85 us (14%)
  starting transfers between devices  28.2 us (4%)
  matrix products  23.9 us (4%)
  between operations  13.6 us (2%)
    psum x1, waiting for transfers between devices, body(): own_vals = lax.psum(picked_part.astype(jnp.bfloat16), 'band')  255 us
    unnamed x11, local copies, waits for them, and re-layouts  113 us
    all_gather x1, blocking collectives, body(): src_vals = lax.all_gather(src_block, 'band', axis=0, tiled=True)  61.5 us
    all_to_all x3, local copies, waits for them, and re-layouts, body(): lax.all_to_all(resident, 'band', split_axis=2, concat_axis=0, tiled=True)  35.3 us
    all_to_all x1, waiting for transfers between devices, body(): lax.all_to_all(resident, 'band', split_axis=2, concat_axis=0, tiled=True)  32.6 us
    all_gather x1, blocking collectives, matched_values(): shard_rows = lax.all_gather(own_block[None], 'kgrp', axis=0, tiled=True)  23.5 us
    all_to_all x1, waiting for transfers between devices, body(): lax.all_to_all(sendgrid, 'band', split_axis=0, concat_axis=3, tiled=True)  22.7 us
    dot_general x3, matrix products, axis_pass(): jnp.einsum(form, field, axis_table(length), precision=lax.Precision.HIGHEST)  19.7 us
  transfers between devices with their start and end apart: 3, of which 3 were waited for; matrix products, arithmetic and copies ran while one was open for 0% of the time, Pallas kernels for 0%

commit v1 on v0

v1 whole, which is shorter than its diff:
```python
import math

import jax
import jax.numpy as jnp
import numpy as np
from jax import lax
from jax.experimental import pallas as pl
from jax.experimental.pallas import tpu as pltpu
from jax.sharding import PartitionSpec as P

MESH = pl.DeviceIdType.MESH
F32 = jnp.float32
BF16 = jnp.bfloat16

NZ = 16
NBAND = 32
NGRP = 16
NU = 512
CELLS = 1024

_DZ = [8]
for _k in range(7, 0, -1):
    _DZ += [_k, -_k]
OFFSETS = [(dz, dy) for dz in _DZ for dy in (0, 1)] + [(0, 1)]


def split_table(table):
    high = jnp.asarray(table, F32).astype(BF16)
    low = (jnp.asarray(table, F32) - high.astype(F32)).astype(BF16)
    return high, low


def plane_tables():
    a = np.arange(8)[:, None, None, None, None]
    u = np.arange(4)[None, :, None, None, None]
    z = np.arange(32)[None, None, :, None, None]
    g = np.arange(4)[None, None, None, :, None]
    kz = np.arange(32)[None, None, None, None, :]
    ky = a + 8 * ((g - a) % 4)
    phase = 2.0 * math.pi / 32.0 * ((ky * u + kz * z) % 32)
    cos_t = (np.cos(phase) / 32.0).reshape(8, 128, 128)
    sin_t = (np.sin(phase) / 32.0).reshape(8, 128, 128)
    return np.concatenate([cos_t, sin_t], axis=2)


def line_table():
    kx = np.arange(32)
    phase = 2.0 * math.pi / 32.0 * (kx[:, None] * kx[None, :] % 32)
    cos_t = np.cos(phase) / math.sqrt(32.0)
    sin_t = np.sin(phase) / math.sqrt(32.0)
    full = np.zeros((2, 4, 32, 32, 2, 4))
    for b in range(4):
        full[0, b, :, :, 0, b] = cos_t
        full[0, b, :, :, 1, b] = sin_t
        full[1, b, :, :, 0, b] = -sin_t
        full[1, b, :, :, 1, b] = cos_t
    return full.reshape(256, 256)


def turn(rows, sign):
    shape = rows.shape
    grouped = rows.reshape(shape[0] // 8, 8, shape[1])
    return (pltpu.roll(grouped, 4, 1) * sign).reshape(shape)


def sign_rows(width):
    row = lax.broadcasted_iota(jnp.int32, (1, 8, width), 1)
    return jnp.where(row < 4, 1.0, -1.0).astype(F32)


def gather_points(x_v, pts_ref, vals):
    pts = pts_ref[...]
    tall = lax.broadcasted_iota(jnp.int32, (512, NU), 0)
    row = 2 * (pts >> 7)
    lane = pts & 127
    data = jnp.concatenate([x_v[b].reshape(512, 128) for b in range(4)], axis=1)
    keep = lax.broadcasted_iota(jnp.int32, (128, NU), 0) == lane
    picked = []
    for c in range(2):
        pick = (tall == row + c).astype(F32).astype(BF16)
        lines = lax.dot_general(data, pick, (((0,), (0,)), ((), ())), preferred_element_type=F32)
        for b in range(4):
            part = jnp.where(keep, lines[b * 128:(b + 1) * 128], 0.0)
            picked.append(jnp.sum(part, axis=0, keepdims=True))
    vals[...] = jnp.concatenate(picked, axis=0).astype(BF16)


def own_matrix(yall, yf, amat):
    for n in range(4):
        yf[...] = yall[:, 0, :, n * 128:(n + 1) * 128].astype(F32).reshape(256, 128)
        parts = [yf[pl.ds(k, 32, stride=8), :] for k in range(8)]
        turned = jnp.transpose(jnp.concatenate(parts, axis=0))
        amat[n * 128:(n + 1) * 128] = turned.astype(BF16)
        crossed = jnp.concatenate([-turned[:, 128:], turned[:, :128]], axis=1)
        amat[NU + n * 128:NU + (n + 1) * 128] = crossed.astype(BF16)


def source_matrix(yall, bmat):
    vals = yall[:, 1].astype(F32).reshape(256, NU)
    bmat[:, 0:NU] = (-vals).astype(BF16)
    bmat[:, NU:2 * NU] = turn(vals, sign_rows(NU)).astype(BF16)


def spread_cells(recv, xf, pmat):
    xf[...] = recv[...].astype(F32).reshape(2048, 128)
    for t in range(8):
        for k in range(8):
            c, b = k // 4, k % 4
            rows = xf[pl.ds(b * 16 + 2 * t + c, 32, stride=64), :]
            pmat[k * 32:(k + 1) * 32, t * 128:(t + 1) * 128] = rows.astype(BF16)


def exchange_cells(amat, bmat, pmat, coul, oscr):
    for n in range(4):
        lanes = slice(n * 256, (n + 1) * 256)
        density = jnp.dot(amat[...], pmat[:, lanes], preferred_element_type=F32)
        fit = coul[:, lanes].astype(F32)
        weighted = jnp.concatenate([fit * density[:NU], fit * density[NU:]], axis=0).astype(BF16)
        oscr[:, lanes] = jnp.dot(bmat[...], weighted, preferred_element_type=F32)


def plane_transform(rows, tab):
    sign = sign_rows(128)
    root = math.sqrt(0.5)
    xs = [rows[:, t * 128:(t + 1) * 128] for t in range(8)]
    even = [xs[t] + xs[t + 4] for t in range(4)]
    odd = [xs[t] - xs[t + 4] for t in range(4)]
    tiles = [None] * 8

    def four(f, first):
        s0, s1, d0 = f[0] + f[2], f[1] + f[3], f[0] - f[2]
        d1 = turn(f[1] - f[3], sign)
        tiles[first] = s0 + s1
        tiles[first + 4] = s0 - s1
        tiles[first + 2] = d0 + d1
        tiles[first + 6] = d0 - d1

    four(even, 0)
    four([
        odd[0],
        (odd[1] + turn(odd[1], sign)) * root,
        turn(odd[2], sign),
        (turn(odd[3], sign) - odd[3]) * root,
    ], 1)
    done = []
    for a in range(8):
        tile = tiles[a].astype(BF16)
        both = jnp.dot(tile, tab[0, a], preferred_element_type=F32)
        both = both + jnp.dot(tile, tab[1, a], preferred_element_type=F32)
        done.append(both[:, :128] + turn(both[:, 128:], sign))
    group = lax.broadcasted_iota(jnp.int32, done[0].shape, 1) >> 5
    outs = []
    for top in range(8):
        half, high = 4 * (top % 2), top // 2
        take = done[half + (0 - high) % 4]
        for g in range(1, 4):
            take = jnp.where(group == g, done[half + (g - high) % 4], take)
        outs.append(pltpu.roll(take, (128 - 32 * high) % 128, 1) if high else take)
    return jnp.concatenate(outs, axis=1)


def line_transform(rz, fx, of, out_ref):
    rows = rz[...].astype(F32).reshape(256, CELLS).astype(BF16)
    full = jnp.dot(fx[0], rows, preferred_element_type=F32)
    full = full + jnp.dot(fx[1], rows, preferred_element_type=F32)
    for t in range(8):
        for p in range(2):
            of[pl.ds(2 * t + p, 128, stride=16), :] = full[p * 128:(p + 1) * 128, t * 128:(t + 1) * 128]
    out_ref[...] = of[...].reshape(4, 32, 16, 128).astype(BF16)


def kernel(x_hbm, pts_ref, partner_ref, coul_hbm, tab_hbm, fx_hbm, out_ref,
           x_v, coul, tab, fx, recv, vals, kbuf, yall, yf, xf, pmat, amat, bmat, oscr, zs, rz, of,
           lsem, asend, arecv, ksend, krecv, psend, precv, msend, mrecv, ysend, yrecv, bsend, brecv):
    me_g = lax.axis_index("kgrp")
    me = lax.axis_index("band")
    z, y = me // 2, me % 2

    def at(dz, dy):
        return ((z + dz + NZ) % NZ) * 2 + (y + dy) % 2

    local = [
        pltpu.make_async_copy(src, dst, lsem.at[n])
        for n, (src, dst) in enumerate(((x_hbm, x_v), (coul_hbm, coul), (tab_hbm, tab), (fx_hbm, fx)))
    ]
    for copy in local:
        copy.start()
    barrier = pltpu.get_barrier_semaphore()

    @pl.loop(1, NBAND)
    def _(k):
        pl.semaphore_signal(barrier, inc=1, device_id={"band": (me + k) % NBAND}, device_id_type=MESH)

    @pl.loop(1, NGRP)
    def _(k):
        pl.semaphore_signal(barrier, inc=1, device_id={"kgrp": (me_g + k) % NGRP}, device_id_type=MESH)

    local[0].wait()
    gather_points(x_v, pts_ref, vals)
    kbuf[me_g] = vals[...]
    yall[me, 0] = vals[...]
    pl.semaphore_wait(barrier, NBAND + NGRP - 2)

    @pl.loop(1, NGRP)
    def _(k):
        pltpu.make_async_remote_copy(
            vals, kbuf.at[me_g], ksend, krecv,
            device_id={"kgrp": (me_g + k) % NGRP}, device_id_type=MESH).start()

    def send_cells(dz, dy):
        to = at(dz, dy)
        pltpu.make_async_remote_copy(
            x_v.at[:, to], recv.at[me], asend, arecv, device_id={"band": to}, device_id_type=MESH).start()

    pltpu.make_async_copy(x_v.at[:, me], recv.at[me], arecv).start()
    for dz, dy in OFFSETS[:7]:
        send_cells(dz, dy)

    pltpu.make_async_copy(kbuf.at[0:NGRP - 1], kbuf.at[0:NGRP - 1], krecv).wait()
    source = jnp.zeros((8, NU), F32)
    for g in range(NGRP):
        hit = jnp.where(partner_ref[g] == me_g, 1.0, 0.0).astype(F32)
        source = source + hit * kbuf[g].astype(F32)
    yall[me, 1] = source.astype(BF16)

    def pass_on(slot, dz, dy, send, arrive):
        pltpu.make_async_remote_copy(
            yall.at[slot], yall.at[slot], send, arrive,
            device_id={"band": at(dz, dy)}, device_id_type=MESH).start()

    def arrived(slot, sem):
        pltpu.make_async_copy(yall.at[slot], yall.at[slot], sem).wait()

    pass_on(me, 1, 0, psend.at[0], precv.at[0])
    pass_on(me, -1, 0, msend.at[0], mrecv.at[0])
    pass_on(me, 0, 1, ysend, yrecv)
    for step in range(1, 9):
        slot = at(-step, 0)
        arrived(slot, precv.at[step - 1])
        if step < 8:
            pass_on(slot, 1, 0, psend.at[step], precv.at[step])
        pass_on(slot, 0, 1, ysend, yrecv)
        if step < 8:
            slot = at(step, 0)
            arrived(slot, mrecv.at[step - 1])
            if step < 7:
                pass_on(slot, -1, 0, msend.at[step], mrecv.at[step])
            pass_on(slot, 0, 1, ysend, yrecv)
        for dz, dy in OFFSETS[4 + 3 * step:7 + 3 * step]:
            send_cells(dz, dy)
    pltpu.make_async_copy(yall.at[0:NZ], yall.at[0:NZ], yrecv).wait()
    own_matrix(yall, yf, amat)
    source_matrix(yall, bmat)

    pltpu.make_async_copy(recv, recv, arecv).wait()
    spread_cells(recv, xf, pmat)
    local[1].wait()
    exchange_cells(amat, bmat, pmat, coul, oscr)
    local[2].wait()

    @pl.loop(0, 4)
    def _(n):
        j = (me // 8 + 2 + n) % 4
        rows = oscr[pl.ds(pl.multiple_of(j * 64, 64), 64), :]
        block = plane_transform(rows, tab).reshape(8, 8, CELLS).astype(BF16)
        zs[pl.ds(j * 8, 8)] = block
        for k in range(8):
            to = j * 8 + k

            @pl.when(to != me)
            def _():
                pltpu.make_async_remote_copy(
                    zs.at[to], rz.at[me], bsend, brecv, device_id={"band": to}, device_id_type=MESH).start()

            @pl.when(to == me)
            def _():
                pltpu.make_async_copy(zs.at[to], rz.at[me], brecv).start()

    local[3].wait()
    pltpu.make_async_copy(rz, rz, brecv).wait()
    line_transform(rz, fx, of, out_ref)

    pltpu.make_async_copy(kbuf.at[0:NGRP - 1], kbuf.at[0:NGRP - 1], ksend).wait()
    pltpu.make_async_copy(recv.at[0:NBAND - 1], recv.at[0:NBAND - 1], asend).wait()
    pltpu.make_async_copy(yall.at[0:NZ], yall.at[0:NZ], ysend).wait()
    for step in range(8):
        arrived(0, psend.at[step])
        if step < 7:
            arrived(0, msend.at[step])
    pltpu.make_async_copy(rz.at[0:NBAND - 1], rz.at[0:NBAND - 1], bsend).wait()


def body(orbitals, points, partner, coulomb):
    tab = jnp.stack(split_table(plane_tables()))
    fx = jnp.stack(split_table(line_table()))
    view = orbitals[0].reshape(4, 2, 32, 8, 128).transpose(0, 2, 3, 1, 4).reshape(4, 32, 16, 128)
    hbm = pl.BlockSpec(memory_space=pl.ANY)
    vmem = pl.BlockSpec(memory_space=pltpu.VMEM)
    dma = pltpu.SemaphoreType.DMA
    out = pl.pallas_call(
        kernel,
        out_shape=jax.ShapeDtypeStruct((4, 32, 16, 128), BF16),
        in_specs=[hbm, vmem, pl.BlockSpec(memory_space=pltpu.SMEM), hbm, hbm, hbm],
        out_specs=vmem,
        scratch_shapes=[
            pltpu.VMEM((4, 32, 16, 128), BF16),
            pltpu.VMEM((NU, CELLS), BF16),
            pltpu.VMEM((2, 8, 128, 256), BF16),
            pltpu.VMEM((2, 256, 256), BF16),
            pltpu.VMEM((NBAND, 4, 16, 128), BF16),
            pltpu.VMEM((8, NU), BF16),
            pltpu.VMEM((NGRP, 8, NU), BF16),
            pltpu.VMEM((NBAND, 2, 8, NU), BF16),
            pltpu.VMEM((256, 128), F32),
            pltpu.VMEM((2048, 128), F32),
            pltpu.VMEM((256, CELLS), BF16),
            pltpu.VMEM((2 * NU, 256), BF16),
            pltpu.VMEM((256, 2 * NU), BF16),
            pltpu.VMEM((256, CELLS), F32),
            pltpu.VMEM((NBAND, 8, CELLS), BF16),
            pltpu.VMEM((NBAND, 8, CELLS), BF16),
            pltpu.VMEM((2048, 128), F32),
            dma((4,)), dma, dma, dma, dma, dma((8,)), dma((8,)), dma((8,)), dma((8,)), dma, dma, dma, dma,
        ],
        compiler_params=pltpu.CompilerParams(
            collective_id=0, has_side_effects=True, vmem_limit_bytes=56 << 20),
    )(view, points.reshape(1, NU), partner, coulomb, tab, fx)
    out = out.reshape(4, 32, 8, 2, 128).transpose(0, 3, 1, 2, 4)
    return out.reshape(1, 4, 2, 32768)


def solution(mesh):
    return jax.shard_map(
        body,
        mesh=mesh,
        in_specs=(P("kgrp", "band", None, None), P(), P(), P(None, "band")),
        out_specs=P("kgrp", "band", None, None),
        check_vma=False,
    )
```

time: 629 us -> 81.7 us (0.13)
  the two profiles are of different devices: /device:TPU:8 before, /device:TPU:22 now
where the time goes in v1:
time: 81.7 us; the launch traced here: 81.5 us
  Pallas kernels  79.3 us (97%)
  local copies, waits for them, and re-layouts  2.2 us (3%)
    pallas_call x1, Pallas kernels, body(): pl.pallas_call(kernel, out_shape=jax.ShapeDtypeStruct((4, 32, 16, 128), B...  79.3 us
    unnamed x1, local copies, waits for them, and re-layouts  2.2 us

profile of v1, /device:TPU:22, one launch (start us, length us, event | category | flops | bytes accessed | tf_op | source)
XLA Modules:
  0.0 81.5 jit_solution(14836855237839112808)
XLA Ops:
  0.0 79.3 %shard_map.82 = bf16[4,32,16,128]{3,2,1,0:T(8,128)(2,1)} custom-call(bf16[4,32,16,128]{3,2,1,0:T(8,128)(2,1)} %bitcast.12, s32[1,512]{1,0:T(1,128)} %bitcast.13, s32[16]{0:T(128)} %partner_ref.1, bf16[512,1024]{1,0:T(8,128)(2,1)} %coul_hbm.1, bf16[2,8,128,256]{3,2,1,0:T(8,128)(2,1)} %constant.13.tab_hbm, bf16[2,256,256]{2,1,0:T(8,128)(2,1)} %constant.20.fx_hbm), custom_call_target="tpu_custom_call" | custom-call | tf_op jit(solution)/shard_map/pallas_call | solution.py:300
  79.3 2.2 %copy.12 = bf16[1,4,2,32768]{3,2,1,0:T(2,128)(2,1)} copy(bf16[1,4,2,32768]{3,2,1,0:T(2,128)(2,1)} %bitcast.11) | data formatting | bytes 1048576

commit v2 on v1

--- a/solution.py
+++ b/solution.py
@@ -18,10 +18,14 @@
 NU = 512
 CELLS = 1024
 
-_DZ = [8]
-for _k in range(7, 0, -1):
-    _DZ += [_k, -_k]
-OFFSETS = [(dz, dy) for dz in _DZ for dy in (0, 1)] + [(0, 1)]
+
+def pairs(*steps):
+    return [(dz, dy) for dz in steps for dy in (0, 1) if (dz, dy) != (0, 0)]
+
+
+NEAR = pairs(0, 1, -1, 2, -2, 3, -3, 4, -4)
+RELAY = [(4, 0), (-4, 0)]
+BATCHES = [pairs(3, -3, 2, -2, 1, -1, 0), pairs(8, 7, -7), pairs(6, -6), pairs(5, -5, 4, -4)]
 
 
 def split_table(table):
@@ -87,7 +91,7 @@
 
 def own_matrix(yall, yf, amat):
     for n in range(4):
-        yf[...] = yall[:, 0, :, n * 128:(n + 1) * 128].astype(F32).reshape(256, 128)
+        yf[...] = yall[:, :, :, 0, :, n * 128:(n + 1) * 128].astype(F32).reshape(256, 128)
         parts = [yf[pl.ds(k, 32, stride=8), :] for k in range(8)]
         turned = jnp.transpose(jnp.concatenate(parts, axis=0))
         amat[n * 128:(n + 1) * 128] = turned.astype(BF16)
@@ -96,7 +100,7 @@
 
 
 def source_matrix(yall, bmat):
-    vals = yall[:, 1].astype(F32).reshape(256, NU)
+    vals = yall[:, :, :, 1].astype(F32).reshape(256, NU)
     bmat[:, 0:NU] = (-vals).astype(BF16)
     bmat[:, NU:2 * NU] = turn(vals, sign_rows(NU)).astype(BF16)
 
@@ -159,7 +163,7 @@
     return jnp.concatenate(outs, axis=1)
 
 
-def line_transform(rz, fx, of, out_ref):
+def line_transform(rz, fx, out_ref, of):
     rows = rz[...].astype(F32).reshape(256, CELLS).astype(BF16)
     full = jnp.dot(fx[0], rows, preferred_element_type=F32)
     full = full + jnp.dot(fx[1], rows, preferred_element_type=F32)
@@ -169,9 +173,9 @@
     out_ref[...] = of[...].reshape(4, 32, 16, 128).astype(BF16)
 
 
-def kernel(x_hbm, pts_ref, partner_ref, coul_hbm, tab_hbm, fx_hbm, out_ref,
-           x_v, coul, tab, fx, recv, vals, kbuf, yall, yf, xf, pmat, amat, bmat, oscr, zs, rz, of,
-           lsem, asend, arecv, ksend, krecv, psend, precv, msend, mrecv, ysend, yrecv, bsend, brecv):
+def kernel(x_hbm, pts_ref, partner_ref, coul_hbm, tab_hbm, rz,
+           x_v, coul, tab, recv, vals, kbuf, yall, yf, xf, pmat, amat, bmat, oscr, zs,
+           lsem, far, asend, arecv, ksend, krecv, gsend, near_recv, group_recv, ysend, yrecv, bsend, brecv):
     me_g = lax.axis_index("kgrp")
     me = lax.axis_index("band")
     z, y = me // 2, me % 2
@@ -179,17 +183,23 @@
     def at(dz, dy):
         return ((z + dz + NZ) % NZ) * 2 + (y + dy) % 2
 
+    def band_copy(src, dst, send, arrive, to):
+        return pltpu.make_async_remote_copy(
+            src, dst, send, arrive, device_id={"band": to}, device_id_type=MESH)
+
+    def await_bytes(ref, sem):
+        pltpu.make_async_copy(ref, ref, sem).wait()
+
     local = [
         pltpu.make_async_copy(src, dst, lsem.at[n])
-        for n, (src, dst) in enumerate(((x_hbm, x_v), (coul_hbm, coul), (tab_hbm, tab), (fx_hbm, fx)))
+        for n, (src, dst) in enumerate(((x_hbm, x_v), (coul_hbm, coul), (tab_hbm, tab)))
     ]
     for copy in local:
         copy.start()
     barrier = pltpu.get_barrier_semaphore()
 
-    @pl.loop(1, NBAND)
-    def _(k):
-        pl.semaphore_signal(barrier, inc=1, device_id={"band": (me + k) % NBAND}, device_id_type=MESH)
+    for dz, dy in NEAR:
+        pl.semaphore_signal(barrier, inc=1, device_id={"band": at(dz, dy)}, device_id_type=MESH)
 
     @pl.loop(1, NGRP)
     def _(k):
@@ -197,9 +207,9 @@
 
     local[0].wait()
     gather_points(x_v, pts_ref, vals)
-    kbuf[me_g] = vals[...]
-    yall[me, 0] = vals[...]
-    pl.semaphore_wait(barrier, NBAND + NGRP - 2)
+    pl.semaphore_wait(barrier, len(NEAR) + NGRP - 1)
+    for dz, dy in RELAY:
+        pl.semaphore_signal(far, inc=1, device_id={"band": at(dz, dy)}, device_id_type=MESH)
 
     @pl.loop(1, NGRP)
     def _(k):
@@ -207,52 +217,46 @@
             vals, kbuf.at[me_g], ksend, krecv,
             device_id={"kgrp": (me_g + k) % NGRP}, device_id_type=MESH).start()
 
-    def send_cells(dz, dy):
-        to = at(dz, dy)
-        pltpu.make_async_remote_copy(
-            x_v.at[:, to], recv.at[me], asend, arecv, device_id={"band": to}, device_id_type=MESH).start()
-
+    def send_cells(offsets):
+        for dz, dy in offsets:
+            to = at(dz, dy)
+            band_copy(x_v.at[:, to], recv.at[me], asend, arecv, to).start()
+
+    send_cells(BATCHES[0])
     pltpu.make_async_copy(x_v.at[:, me], recv.at[me], arecv).start()
-    for dz, dy in OFFSETS[:7]:
-        send_cells(dz, dy)
-
-    pltpu.make_async_copy(kbuf.at[0:NGRP - 1], kbuf.at[0:NGRP - 1], krecv).wait()
+    if RELAY:
+        pl.semaphore_wait(far, len(RELAY))
+    send_cells(BATCHES[1])
+
+    inner, outer = z % 4, z // 4
+    kbuf[me_g] = vals[...]
+    yall[outer, inner, y, 0] = vals[...]
+    await_bytes(kbuf.at[0:NGRP - 1], krecv)
     source = jnp.zeros((8, NU), F32)
     for g in range(NGRP):
         hit = jnp.where(partner_ref[g] == me_g, 1.0, 0.0).astype(F32)
         source = source + hit * kbuf[g].astype(F32)
-    yall[me, 1] = source.astype(BF16)
-
-    def pass_on(slot, dz, dy, send, arrive):
-        pltpu.make_async_remote_copy(
-            yall.at[slot], yall.at[slot], send, arrive,
-            device_id={"band": at(dz, dy)}, device_id_type=MESH).start()
-
-    def arrived(slot, sem):
-        pltpu.make_async_copy(yall.at[slot], yall.at[slot], sem).wait()
-
-    pass_on(me, 1, 0, psend.at[0], precv.at[0])
-    pass_on(me, -1, 0, msend.at[0], mrecv.at[0])
-    pass_on(me, 0, 1, ysend, yrecv)
-    for step in range(1, 9):
-        slot = at(-step, 0)
-        arrived(slot, precv.at[step - 1])
-        if step < 8:
-            pass_on(slot, 1, 0, psend.at[step], precv.at[step])
-        pass_on(slot, 0, 1, ysend, yrecv)
-        if step < 8:
-            slot = at(step, 0)
-            arrived(slot, mrecv.at[step - 1])
-            if step < 7:
-                pass_on(slot, -1, 0, msend.at[step], mrecv.at[step])
-            pass_on(slot, 0, 1, ysend, yrecv)
-        for dz, dy in OFFSETS[4 + 3 * step:7 + 3 * step]:
-            send_cells(dz, dy)
-    pltpu.make_async_copy(yall.at[0:NZ], yall.at[0:NZ], yrecv).wait()
+    yall[outer, inner, y, 1] = source.astype(BF16)
+
+    mine = yall.at[outer, inner, y]
+    for dz in (8, 4, -4):
+        band_copy(mine, mine, gsend, near_recv, at(dz, 0)).start()
+    send_cells(BATCHES[2])
+    await_bytes(yall.at[0, 0:3, 0], near_recv)
+    group = yall.at[:, inner, y]
+    for n, dz in enumerate((2, 1, -1)):
+        band_copy(group, group, gsend, group_recv.at[n], at(dz, 0)).start()
+    band_copy(group, group, ysend, yrecv, at(0, 1)).start()
+    send_cells(BATCHES[3])
+    for n, dz in ((1, -1), (2, 1), (0, -2)):
+        await_bytes(yall.at[:, 0, 0], group_recv.at[n])
+        other = yall.at[:, (inner + dz + 4) % 4, y]
+        band_copy(other, other, ysend, yrecv, at(0, 1)).start()
+    await_bytes(yall.at[:, :, 0], yrecv)
     own_matrix(yall, yf, amat)
     source_matrix(yall, bmat)
 
-    pltpu.make_async_copy(recv, recv, arecv).wait()
+    await_bytes(recv, arecv)
     spread_cells(recv, xf, pmat)
     local[1].wait()
     exchange_cells(amat, bmat, pmat, coul, oscr)
@@ -269,25 +273,19 @@
 
             @pl.when(to != me)
             def _():
-                pltpu.make_async_remote_copy(
-                    zs.at[to], rz.at[me], bsend, brecv, device_id={"band": to}, device_id_type=MESH).start()
+                band_copy(zs.at[to], rz.at[me], bsend, brecv, to).start()
 
             @pl.when(to == me)
             def _():
                 pltpu.make_async_copy(zs.at[to], rz.at[me], brecv).start()
 
-    local[3].wait()
-    pltpu.make_async_copy(rz, rz, brecv).wait()
-    line_transform(rz, fx, of, out_ref)
-
-    pltpu.make_async_copy(kbuf.at[0:NGRP - 1], kbuf.at[0:NGRP - 1], ksend).wait()
-    pltpu.make_async_copy(recv.at[0:NBAND - 1], recv.at[0:NBAND - 1], asend).wait()
-    pltpu.make_async_copy(yall.at[0:NZ], yall.at[0:NZ], ysend).wait()
-    for step in range(8):
-        arrived(0, psend.at[step])
-        if step < 7:
-            arrived(0, msend.at[step])
-    pltpu.make_async_copy(rz.at[0:NBAND - 1], rz.at[0:NBAND - 1], bsend).wait()
+    await_bytes(kbuf.at[0:NGRP - 1], ksend)
+    await_bytes(recv.at[0:NBAND - 1], asend)
+    await_bytes(yall.at[0, 0:3, 0], gsend)
+    await_bytes(yall.at[:, 0:3, 0], gsend)
+    await_bytes(yall.at[:, :, 0], ysend)
+    await_bytes(rz, brecv)
+    await_bytes(rz.at[0:NBAND - 1], bsend)
 
 
 def body(orbitals, points, partner, coulomb):
@@ -297,20 +295,19 @@
     hbm = pl.BlockSpec(memory_space=pl.ANY)
     vmem = pl.BlockSpec(memory_space=pltpu.VMEM)
     dma = pltpu.SemaphoreType.DMA
-    out = pl.pallas_call(
+    lines = pl.pallas_call(
         kernel,
-        out_shape=jax.ShapeDtypeStruct((4, 32, 16, 128), BF16),
-        in_specs=[hbm, vmem, pl.BlockSpec(memory_space=pltpu.SMEM), hbm, hbm, hbm],
-        out_specs=vmem,
+        out_shape=jax.ShapeDtypeStruct((NBAND, 8, CELLS), BF16),
+        in_specs=[hbm, vmem, pl.BlockSpec(memory_space=pltpu.SMEM), hbm, hbm],
+        out_specs=hbm,
         scratch_shapes=[
             pltpu.VMEM((4, 32, 16, 128), BF16),
             pltpu.VMEM((NU, CELLS), BF16),
             pltpu.VMEM((2, 8, 128, 256), BF16),
-            pltpu.VMEM((2, 256, 256), BF16),
             pltpu.VMEM((NBAND, 4, 16, 128), BF16),
             pltpu.VMEM((8, NU), BF16),
             pltpu.VMEM((NGRP, 8, NU), BF16),
-            pltpu.VMEM((NBAND, 2, 8, NU), BF16),
+            pltpu.VMEM((4, 4, 2, 2, 8, NU), BF16),
             pltpu.VMEM((256, 128), F32),
             pltpu.VMEM((2048, 128), F32),
             pltpu.VMEM((256, CELLS), BF16),
@@ -318,13 +315,19 @@
             pltpu.VMEM((256, 2 * NU), BF16),
             pltpu.VMEM((256, CELLS), F32),
             pltpu.VMEM((NBAND, 8, CELLS), BF16),
-            pltpu.VMEM((NBAND, 8, CELLS), BF16),
-            pltpu.VMEM((2048, 128), F32),
-            dma((4,)), dma, dma, dma, dma, dma((8,)), dma((8,)), dma((8,)), dma((8,)), dma, dma, dma, dma,
+            dma((3,)), pltpu.SemaphoreType.REGULAR, dma, dma, dma, dma, dma, dma, dma((3,)), dma, dma, dma, dma,
         ],
         compiler_params=pltpu.CompilerParams(
-            collective_id=0, has_side_effects=True, vmem_limit_bytes=56 << 20),
-    )(view, points.reshape(1, NU), partner, coulomb, tab, fx)
+            collective_id=0, has_side_effects=True, vmem_limit_bytes=60 << 20),
+    )(view, points.reshape(1, NU), partner, coulomb, tab)
+    out = pl.pallas_call(
+        line_transform,
+        out_shape=jax.ShapeDtypeStruct((4, 32, 16, 128), BF16),
+        in_specs=[vmem, vmem],
+        out_specs=vmem,
+        scratch_shapes=[pltpu.VMEM((2048, 128), F32)],
+        compiler_params=pltpu.CompilerParams(vmem_limit_bytes=16 << 20),
+    )(lines, fx)
     out = out.reshape(4, 32, 8, 2, 128).transpose(0, 3, 1, 2, 4)
     return out.reshape(1, 4, 2, 32768)
 

time: 81.7 us -> 75.7 us (0.927)
  the two profiles are of different devices: /device:TPU:22 before, /device:TPU:98 now
where the time goes in v2:
time: 75.7 us; the launch traced here: 75.6 us
  Pallas kernels  74.5 us (98%)
  local copies, waits for them, and re-layouts  1.04 us (1%)
    pallas_call x1, Pallas kernels, body(): pl.pallas_call(kernel, out_shape=jax.ShapeDtypeStruct((NBAND, 8, CELLS),...  73.1 us

profile of v2, /device:TPU:98, one launch (start us, length us, event | category | flops | bytes accessed | tf_op | source)
XLA Modules:
  0.0 75.6 jit_solution(105373766542242115)
XLA Ops:
  0.0 0.0 copy-start.1
  0.0 73.1 %shard_map.82.rz = bf16[32,8,1024]{2,1,0:T(8,128)(2,1)} custom-call(bf16[4,32,16,128]{3,2,1,0:T(8,128)(2,1)} %bitcast.11, s32[1,512]{1,0:T(1,128)} %bitcast.12, s32[16]{0:T(128)} %partner_ref.1, bf16[512,1024]{1,0:T(8,128)(2,1)} %coul_hbm.1, bf16[2,8,128,256]{3,2,1,0:T(8,128)(2,1)} %constant.13.tab_hbm), custom_call_target="tpu_custom_call" | custom-call | tf_op jit(solution)/shard_map/pallas_call | solution.py:298
  73.1 0.0 copy-done.1
  73.1 0.0 copy-start
  73.1 1.0 %copy-done = bf16[32,8,1024]{2,1,0:T(8,128)(2,1)S(1)} copy-done((bf16[32,8,1024]{2,1,0:T(8,128)(2,1)S(1)}, bf16[32,8,1024]{2,1,0:T(8,128)(2,1)}, u32[]{:S(2)}) %copy-start) | copy-done | bytes 524312
  74.1 1.4 %shard_map.83 = bf16[4,32,16,128]{3,2,1,0:T(8,128)(2,1)} custom-call(bf16[32,8,1024]{2,1,0:T(8,128)(2,1)S(1)} %copy-done, bf16[2,256,256]{2,1,0:T(8,128)(2,1)S(1)} %copy-done.1), custom_call_target="tpu_custom_call" | custom-call | tf_op jit(solution)/shard_map/pallas_call | solution.py:323
Async XLA Ops:
  0.0 73.1 %copy-start.1 = (bf16[2,256,256]{2,1,0:T(8,128)(2,1)S(1)}, bf16[2,256,256]{2,1,0:T(8,128)(2,1)}, u32[]{:S(2)}) copy-start(bf16[2,256,256]{2,1,0:T(8,128)(2,1)} %constant.20.fx) | copy-start | bytes 786436
  73.1 1.0 %copy-start = (bf16[32,8,1024]{2,1,0:T(8,128)(2,1)S(1)}, bf16[32,8,1024]{2,1,0:T(8,128)(2,1)}, u32[]{:S(2)}) copy-start(bf16[32,8,1024]{2,1,0:T(8,128)(2,1)} %shard_map.82.rz) | copy-start | bytes 1572868

commit v3 on v2

--- a/solution.py
+++ b/solution.py
@@ -23,7 +23,7 @@
     return [(dz, dy) for dz in steps for dy in (0, 1) if (dz, dy) != (0, 0)]
 
 
-NEAR = pairs(0, 1, -1, 2, -2, 3, -3, 4, -4)
+NEAR = pairs(4, -4, 3, -3, 2, -2, 1, -1, 0)
 RELAY = [(4, 0), (-4, 0)]
 BATCHES = [pairs(3, -3, 2, -2, 1, -1, 0), pairs(8, 7, -7), pairs(6, -6), pairs(5, -5, 4, -4)]
 
@@ -244,11 +244,14 @@
     send_cells(BATCHES[2])
     await_bytes(yall.at[0, 0:3, 0], near_recv)
     group = yall.at[:, inner, y]
-    for n, dz in enumerate((2, 1, -1)):
+    for n, dz in enumerate((1, -1)):
         band_copy(group, group, gsend, group_recv.at[n], at(dz, 0)).start()
+    for n, dz in enumerate((2, -2)):
+        half = yall.at[2 * n:2 * n + 2, inner, y]
+        band_copy(half, half, gsend, group_recv.at[2], at(dz, 0)).start()
     band_copy(group, group, ysend, yrecv, at(0, 1)).start()
     send_cells(BATCHES[3])
-    for n, dz in ((1, -1), (2, 1), (0, -2)):
+    for n, dz in enumerate((-1, 1, 2)):
         await_bytes(yall.at[:, 0, 0], group_recv.at[n])
         other = yall.at[:, (inner + dz + 4) % 4, y]
         band_copy(other, other, ysend, yrecv, at(0, 1)).start()

time: 75.7 us -> 74.1 us (0.979)
  the two profiles are of different devices: /device:TPU:98 before, /device:TPU:104 now
where the time goes in v3:
time: 74.1 us; the launch traced here: 73.9 us
  Pallas kernels  72.8 us (98%)
  local copies, waits for them, and re-layouts  1.04 us (1%)
    pallas_call x1, Pallas kernels, body(): pl.pallas_call(kernel, out_shape=jax.ShapeDtypeStruct((NBAND, 8, CELLS),...  71.4 us

profile of v3, /device:TPU:104, one launch (start us, length us, event | category | flops | bytes accessed | tf_op | source)
XLA Modules:
  0.0 73.9 jit_solution(9929851219721792973)
XLA Ops:
  0.0 0.0 copy-start.1
  0.0 71.4 %shard_map.82.rz = bf16[32,8,1024]{2,1,0:T(8,128)(2,1)} custom-call(bf16[4,32,16,128]{3,2,1,0:T(8,128)(2,1)} %bitcast.11, s32[1,512]{1,0:T(1,128)} %bitcast.12, s32[16]{0:T(128)} %partner_ref.1, bf16[512,1024]{1,0:T(8,128)(2,1)} %coul_hbm.1, bf16[2,8,128,256]{3,2,1,0:T(8,128)(2,1)} %constant.13.tab_hbm), custom_call_target="tpu_custom_call" | custom-call | tf_op jit(solution)/shard_map/pallas_call | solution.py:301
  71.4 0.0 copy-done.1
  71.4 0.0 copy-start
  71.4 1.0 %copy-done = bf16[32,8,1024]{2,1,0:T(8,128)(2,1)S(1)} copy-done((bf16[32,8,1024]{2,1,0:T(8,128)(2,1)S(1)}, bf16[32,8,1024]{2,1,0:T(8,128)(2,1)}, u32[]{:S(2)}) %copy-start) | copy-done | bytes 524312
  72.5 1.4 %shard_map.83 = bf16[4,32,16,128]{3,2,1,0:T(8,128)(2,1)} custom-call(bf16[32,8,1024]{2,1,0:T(8,128)(2,1)S(1)} %copy-done, bf16[2,256,256]{2,1,0:T(8,128)(2,1)S(1)} %copy-done.1), custom_call_target="tpu_custom_call" | custom-call | tf_op jit(solution)/shard_map/pallas_call | solution.py:326
Async XLA Ops:
  0.0 71.4 %copy-start.1 = (bf16[2,256,256]{2,1,0:T(8,128)(2,1)S(1)}, bf16[2,256,256]{2,1,0:T(8,128)(2,1)}, u32[]{:S(2)}) copy-start(bf16[2,256,256]{2,1,0:T(8,128)(2,1)} %constant.20.fx) | copy-start | bytes 786436
  71.4 1.0 %copy-start = (bf16[32,8,1024]{2,1,0:T(8,128)(2,1)S(1)}, bf16[32,8,1024]{2,1,0:T(8,128)(2,1)}, u32[]{:S(2)}) copy-start(bf16[32,8,1024]{2,1,0:T(8,128)(2,1)} %shard_map.82.rz) | copy-start | bytes 1572868

commit v4 on v3

--- a/solution.py
+++ b/solution.py
@@ -194,8 +194,6 @@
         pltpu.make_async_copy(src, dst, lsem.at[n])
         for n, (src, dst) in enumerate(((x_hbm, x_v), (coul_hbm, coul), (tab_hbm, tab)))
     ]
-    for copy in local:
-        copy.start()
     barrier = pltpu.get_barrier_semaphore()
 
     for dz, dy in NEAR:
@@ -205,8 +203,14 @@
     def _(k):
         pl.semaphore_signal(barrier, inc=1, device_id={"kgrp": (me_g + k) % NGRP}, device_id_type=MESH)
 
+    for copy in local:
+        copy.start()
     local[0].wait()
+    pltpu.make_async_copy(x_v.at[:, me], recv.at[me], arecv).start()
     gather_points(x_v, pts_ref, vals)
+    inner, outer = z % 4, z // 4
+    kbuf[me_g] = vals[...]
+    yall[outer, inner, y, 0] = vals[...]
     pl.semaphore_wait(barrier, len(NEAR) + NGRP - 1)
     for dz, dy in RELAY:
         pl.semaphore_signal(far, inc=1, device_id={"band": at(dz, dy)}, device_id_type=MESH)
@@ -223,14 +227,10 @@
             band_copy(x_v.at[:, to], recv.at[me], asend, arecv, to).start()
 
     send_cells(BATCHES[0])
-    pltpu.make_async_copy(x_v.at[:, me], recv.at[me], arecv).start()
     if RELAY:
         pl.semaphore_wait(far, len(RELAY))
     send_cells(BATCHES[1])
 
-    inner, outer = z % 4, z // 4
-    kbuf[me_g] = vals[...]
-    yall[outer, inner, y, 0] = vals[...]
     await_bytes(kbuf.at[0:NGRP - 1], krecv)
     source = jnp.zeros((8, NU), F32)
     for g in range(NGRP):

time: 74.1 us -> 74.5 us (level)
  no operation moved by 1% of the time
where the time goes in v4:
time: 74.5 us; the launch traced here: 74.3 us
  Pallas kernels  73.2 us (98%)
  local copies, waits for them, and re-layouts  1.04 us (1%)
    pallas_call x1, Pallas kernels, body(): pl.pallas_call(kernel, out_shape=jax.ShapeDtypeStruct((NBAND, 8, CELLS),...  71.8 us

profile of v4, /device:TPU:104, one launch (start us, length us, event | category | flops | bytes accessed | tf_op | source)
XLA Modules:
  0.0 74.3 jit_solution(12771286206018655781)
XLA Ops:
  0.0 0.0 copy-start.1
  0.0 71.8 %shard_map.82.rz = bf16[32,8,1024]{2,1,0:T(8,128)(2,1)} custom-call(bf16[4,32,16,128]{3,2,1,0:T(8,128)(2,1)} %bitcast.11, s32[1,512]{1,0:T(1,128)} %bitcast.12, s32[16]{0:T(128)} %partner_ref.1, bf16[512,1024]{1,0:T(8,128)(2,1)} %coul_hbm.1, bf16[2,8,128,256]{3,2,1,0:T(8,128)(2,1)} %constant.13.tab_hbm), custom_call_target="tpu_custom_call" | custom-call | tf_op jit(solution)/shard_map/pallas_call | solution.py:301
  71.8 0.0 copy-done.1
  71.8 0.0 copy-start
  71.8 1.0 %copy-done = bf16[32,8,1024]{2,1,0:T(8,128)(2,1)S(1)} copy-done((bf16[32,8,1024]{2,1,0:T(8,128)(2,1)S(1)}, bf16[32,8,1024]{2,1,0:T(8,128)(2,1)}, u32[]{:S(2)}) %copy-start) | copy-done | bytes 524312
  72.9 1.4 %shard_map.83 = bf16[4,32,16,128]{3,2,1,0:T(8,128)(2,1)} custom-call(bf16[32,8,1024]{2,1,0:T(8,128)(2,1)S(1)} %copy-done, bf16[2,256,256]{2,1,0:T(8,128)(2,1)S(1)} %copy-done.1), custom_call_target="tpu_custom_call" | custom-call | tf_op jit(solution)/shard_map/pallas_call | solution.py:326
Async XLA Ops:
  0.0 71.8 %copy-start.1 = (bf16[2,256,256]{2,1,0:T(8,128)(2,1)S(1)}, bf16[2,256,256]{2,1,0:T(8,128)(2,1)}, u32[]{:S(2)}) copy-start(bf16[2,256,256]{2,1,0:T(8,128)(2,1)} %constant.20.fx) | copy-start | bytes 786436
  71.8 1.0 %copy-start = (bf16[32,8,1024]{2,1,0:T(8,128)(2,1)S(1)}, bf16[32,8,1024]{2,1,0:T(8,128)(2,1)}, u32[]{:S(2)}) copy-start(bf16[32,8,1024]{2,1,0:T(8,128)(2,1)} %shard_map.82.rz) | copy-start | bytes 1572868
